TPU v7x, 256 devices: a whole 4x4x8 slice. The times are simulated.
256 devices in a mesh: dp: 2 (over z_lo), expert: 128 (over y, x, z_hi, core).
Axes of the slice: x: 4, y: 4, z: 8 (z_hi: 4, z_lo: 2; z = z_hi * 2 + z_lo), core: 2. Of those that a mesh axis runs over, the one named last changes fastest.
Arguments:
- tokens: bfloat16 [32768, 4096], P(('dp', 'expert')), may hold values from -6 to 6
- routes: int32 [256, 16, 4], P(('dp', 'expert')), may hold values from 0 to 127, as said below
- gate_values: float32 [256, 16, 4], P(('dp', 'expert')), may hold values from 0.1 to 1
- gate_weight: bfloat16 [128, 4096, 256], P('expert', 'dp'), may hold values from -0.09375 to 0.09375
- up_weight: bfloat16 [128, 4096, 256], P('expert', 'dp'), may hold values from -0.09375 to 0.09375
- down_weight: bfloat16 [128, 4096, 256], P('expert', 'dp'), may hold values from -0.125 to 0.125
- cotangent: bfloat16 [32768, 4096], P(('dp', 'expert')), may hold values from -6 to 6
Outputs:
- layer_out: bfloat16 [32768, 4096], P(('dp', 'expert'))
- token_grad: bfloat16 [32768, 4096], P(('dp', 'expert'))
- gate_grad: bfloat16 [128, 4096, 256], P('expert', 'dp')
- up_grad: bfloat16 [128, 4096, 256], P('expert', 'dp')
- down_grad: bfloat16 [128, 4096, 256], P('expert', 'dp')
Inputs may be any that keep to these rules, and one draw needn't show every extreme that they name: `routes`: for each home block and each expert, 4 distinct positions within that block.
All inputs are finite; a program needn't handle non-finite values.
Results may differ from a plain program's by a relative error of at most 0.025.
Values may be sent and summed in bfloat16 or wider, within the bound.
A program may use at most 128 MiB of HBM per device.

v0:
```python
import jax
import jax.numpy as jnp
from jax import lax
from jax.sharding import Mesh
from jax.sharding import PartitionSpec as P

SPLIT = 8
ROWS = ("dp", "yx", "col")


def send_out(payload):
    arrived = lax.all_to_all(payload, "yx", split_axis=0, concat_axis=0, tiled=True)
    shared = lax.all_gather(arrived, "col", axis=0, tiled=True)
    return shared.reshape(-1, payload.shape[-1])


def bring_back(partial_value, expert_count):
    total_rows, width = partial_value.shape
    summed = lax.psum_scatter(partial_value, "col", scatter_dimension=0, tiled=True)
    summed = summed.reshape(expert_count, -1, width)
    returned = lax.all_to_all(summed, "yx", split_axis=0, concat_axis=0, tiled=True)
    return returned.astype(jnp.float32)


def shards(tokens, routes, gate_values, gate_weight, up_weight, down_weight, cotangent):
    width = tokens.shape[1]
    expert_count = routes.shape[1]
    chosen = routes[0]
    scales = gate_values[0][:, :, None]
    contract_last = (((1,), (1,)), ((), ()))
    contract_first = (((0,), (0,)), ((), ()))
    full_gate, full_up, full_down = (
        lax.all_gather(gate_weight, "dp", axis=1, tiled=True),
        lax.all_gather(up_weight, "dp", axis=1, tiled=True),
        lax.all_gather(down_weight, "dp", axis=1, tiled=True),
    )
    full_gate = full_gate[0]
    full_up = full_up[0]
    full_down = full_down[0]
    token_rows = send_out(tokens[chosen])
    scaled_cot = (scales * cotangent[chosen].astype(jnp.float32)).astype(jnp.bfloat16)
    cot_rows = send_out(scaled_cot)
    gate_pre = jnp.dot(token_rows, full_gate, preferred_element_type=jnp.float32)
    up_pre = jnp.dot(token_rows, full_up, preferred_element_type=jnp.float32)
    gate_sigma = jax.nn.sigmoid(gate_pre)
    hidden = (gate_pre * gate_sigma * up_pre).astype(jnp.bfloat16)
    partial_value = lax.dot_general(
        hidden, full_down, contract_last, preferred_element_type=jnp.float32
    ).astype(jnp.bfloat16)
    combined = bring_back(partial_value, expert_count)
    layer_out = jnp.zeros((tokens.shape[0], width), jnp.float32).at[chosen].add(scales * combined)
    hidden_grad = jnp.dot(cot_rows, full_down, preferred_element_type=jnp.float32)
    gate_rows = (hidden_grad * up_pre * gate_sigma * (1.0 + gate_pre * (1.0 - gate_sigma))).astype(
        jnp.bfloat16
    )
    up_rows = (hidden_grad * gate_pre * gate_sigma).astype(jnp.bfloat16)
    partial_grad = (
        lax.dot_general(gate_rows, full_gate, contract_last, preferred_element_type=jnp.float32)
        + lax.dot_general(up_rows, full_up, contract_last, preferred_element_type=jnp.float32)
    ).astype(jnp.bfloat16)
    token_grad = (
        jnp.zeros((tokens.shape[0], width), jnp.float32)
        .at[chosen]
        .add(bring_back(partial_grad, expert_count))
    )
    grad_sums = lax.psum_scatter(
        jnp.concatenate(
            [
                lax.dot_general(
                    token_rows, gate_rows, contract_first, preferred_element_type=jnp.float32
                ),
                lax.dot_general(
                    token_rows, up_rows, contract_first, preferred_element_type=jnp.float32
                ),
                lax.dot_general(
                    cot_rows, hidden, contract_first, preferred_element_type=jnp.float32
                ),
            ],
            axis=1,
        ).astype(jnp.bfloat16),
        "dp",
        scatter_dimension=0,
        tiled=True,
    ).astype(jnp.float32)
    hidden_width = hidden.shape[1]
    gate_grad = grad_sums[:, :hidden_width].astype(jnp.bfloat16)[None]
    up_grad = grad_sums[:, hidden_width : 2 * hidden_width].astype(jnp.bfloat16)[None]
    down_grad = grad_sums[:, 2 * hidden_width :].astype(jnp.bfloat16)[None]
    return (
        layer_out.astype(jnp.bfloat16),
        token_grad.astype(jnp.bfloat16),
        gate_grad,
        up_grad,
        down_grad,
    )


def solution(mesh):
    n_dp, n_expert = mesh.devices.shape
    fine = Mesh(mesh.devices.reshape(n_dp, n_expert // SPLIT, SPLIT), ROWS)
    placed = (
        P(ROWS, None),
        P(ROWS, None, None),
        P(ROWS, None, None),
        P(("yx", "col"), "dp", None),
        P(("yx", "col"), "dp", None),
        P(("yx", "col"), "dp", None),
        P(ROWS, None),
    )
    return jax.shard_map(
        shards,
        mesh=fine,
        in_specs=placed,
        out_specs=(
            P(ROWS, None),
            P(ROWS, None),
            P(("yx", "col"), "dp", None),
            P(("yx", "col"), "dp", None),
            P(("yx", "col"), "dp", None),
        ),
        check_vma=False,
    )
```

profile of v0, /device:TPU:1, one launch (start us, length us, event | category | flops | bytes accessed | tf_op | source)
XLA Modules:
  0.0 485.7 jit_solution(14935874238161383922)
XLA Ops:
  7.2 0.0 all-gather.6.cloned.1.call-start
  7.2 0.8 compare_select_fusion
  8.1 0.1 copy.22
  8.2 0.1 reshape.73
  8.3 0.2 copy-done
  8.4 0.9 gather_fusion
  9.3 0.2 reshape.56
  9.5 18.0 %all_to_all.20 = bf16[16,4,4096]{2,1,0:T(4,128)(2,1)} all-to-all(bf16[16,4,4096]{2,1,0:T(4,128)(2,1)S(1)} %reshape.56), channel_id=1, replica_groups=mesh['dp'=2,'yx'=16,'col'=8] {'yx'}, dimensions={0} | all-to-all | bytes 1048576 | tf_op jit(solution)/shard_map/all_to_all | solution.py:12
  27.5 0.0 all-gather.6.cloned.1.call-update
  27.5 0.0 all-gather.14.cloned.1.call-start
  27.6 0.1 copy.23
  27.7 0.9 gather_fusion.1
  28.5 0.3 reshape.91
  28.9 0.3 multiply_convert_fusion
  29.2 13.0 %all_to_all.21 = bf16[16,4,4096]{2,1,0:T(4,128)(2,1)} all-to-all(bf16[16,4,4096]{2,1,0:T(4,128)(2,1)S(1)} %multiply_convert_fusion), channel_id=1, replica_groups=mesh['dp'=2,'yx'=16,'col'=8] {'yx'}, dimensions={0} | all-to-all | bytes 1048576 | tf_op jit(solution)/shard_map/all_to_all | solution.py:12
  42.1 0.0 all-gather.14.cloned.1.call-update
  42.2 0.0 all-gather.10.cloned.1.call-start
  42.2 0.7 all-gather.10.cloned.1.call-update
  42.9 0.0 all-gather.8.cloned.1.call-start
  42.9 0.5 all-gather.8.cloned.1.call-update
  43.5 0.0 all-gather.12.cloned.1.call-start
  43.5 0.5 all-gather.12.cloned.1.call-update
  44.1 0.0 reduce-scatter.4.cloned.1.call-start
  44.1 34.5 %all-gather.6.cloned.1.call-done = bf16[128,4,4096]{2,1,0:T(4,128)(2,1)} async-done(((bf16[16,4,4096]{2,1,0:T(4,128)(2,1)}), bf16[128,4,4096]{2,1,0:T(4,128)(2,1)}) %all-gather.6.cloned.1.call-update) | async-done | bytes 4194320 | tf_op jit(solution)/shard_map/all_gather | solution.py:13
  78.6 6.9 %reshape.51 = bf16[512,4096]{1,0:T(8,128)(2,1)} reshape(bf16[128,4,4096]{2,1,0:T(4,128)(2,1)} %all-gather.6.cloned.1.call-done) | data formatting | bytes 8388608 | tf_op jit(solution)/shard_map/reshape | solution.py:14
  85.4 46.2 %all-gather.14.cloned.1.call-done = bf16[128,4,4096]{2,1,0:T(4,128)(2,1)} async-done(((bf16[16,4,4096]{2,1,0:T(4,128)(2,1)}), bf16[128,4,4096]{2,1,0:T(4,128)(2,1)}) %all-gather.14.cloned.1.call-update) | async-done | bytes 4194320 | tf_op jit(solution)/shard_map/all_gather | solution.py:13
  131.6 7.0 %reshape.53 = bf16[512,4096]{1,0:T(8,128)(2,1)} reshape(bf16[128,4,4096]{2,1,0:T(4,128)(2,1)} %all-gather.14.cloned.1.call-done) | data formatting | bytes 8388608 | tf_op jit(solution)/shard_map/reshape | solution.py:14
  138.6 33.8 %all-gather.10.cloned.1.call-done = bf16[1,4096,256]{2,1,0:T(8,128)(2,1)} async-done(((bf16[1,2048,256]{2,1,0:T(8,128)(2,1)}), bf16[1,4096,256]{2,1,0:T(8,128)(2,1)}) %all-gather.10.cloned.1.call-update) | async-done | bytes 2097168 | tf_op jit(solution)/shard_map/all_gather | solution.py:34
  172.4 4.1 fusion.4
  176.5 36.2 %all-gather.8.cloned.1.call-done = bf16[1,4096,256]{2,1,0:T(8,128)(2,1)} async-done(((bf16[1,2048,256]{2,1,0:T(8,128)(2,1)}), bf16[1,4096,256]{2,1,0:T(8,128)(2,1)}) %all-gather.8.cloned.1.call-update) | async-done | bytes 2097168 | tf_op jit(solution)/shard_map/all_gather | solution.py:33
  212.8 4.1 fusion.8
  216.9 36.2 %all-gather.12.cloned.1.call-done = bf16[1,4096,256]{2,1,0:T(8,128)(2,1)} async-done(((bf16[1,2048,256]{2,1,0:T(8,128)(2,1)}), bf16[1,4096,256]{2,1,0:T(8,128)(2,1)}) %all-gather.12.cloned.1.call-update) | async-done | bytes 2097168 | tf_op jit(solution)/shard_map/all_gather | solution.py:35
  253.1 4.4 multiply_convert_fusion.1
  257.5 3.4 convolution_convert_fusion
  260.9 0.0 reduce-scatter.6.cloned.1.call-start
  261.0 1.5 copy-done.5
  262.5 1.3 fusion.6
  263.8 0.3 copy-done.4
  264.1 3.3 add_convert_fusion
  267.3 0.0 reduce-scatter.6.cloned.1.call-update
  267.4 0.2 reduce-scatter.8.cloned.1.call-start
  267.6 3.6 convolution_convert_fusion.1
  271.3 1.4 convolution_convert_fusion.2
  272.6 1.4 convolution_convert_fusion.3
  274.0 9.4 %pad_maximum_fusion = bf16[4096,768]{0,1:T(8,128)(2,1)} fusion(bf16[4096,256]{0,1:T(8,128)(2,1)S(1)} %convolution_convert_fusion.1, bf16[4096,256]{0,1:T(8,128)(2,1)S(1)} %convolution_convert_fusion.2, bf16[4096,256]{0,1:T(8,128)(2,1)S(1)} %convolution_convert_fusion.3), kind=kLoop, calls=%fused_computation.5 | loop fusion | flops 18874368 | bytes 12582912 | tf_op jit(solution)/shard_map/concatenate | solution.py:67
  283.4 36.0 %reduce-scatter.4.cloned.1.call-done = bf16[64,4096]{1,0:T(8,128)(2,1)} async-done(((bf16[512,4096]{1,0:T(8,128)(2,1)}), bf16[64,4096]{1,0:T(8,128)(2,1)}) %reduce-scatter.4.cloned.1.call-update) | async-done | bytes 524304 | tf_op jit(solution)/shard_map/reduce_scatter | solution.py:19
  319.4 2.0 reshape.52
  321.4 6.1 %all-to-all-start.1 = ((bf16[16,4,4096]{2,1,0:T(4,128)(2,1)}), bf16[16,4,4096]{2,1,0:T(4,128)(2,1)S(1)}, u32[]{:S(2)}, u32[]{:S(2)}) async-start(bf16[16,4,4096]{2,1,0:T(4,128)(2,1)} %reshape.52), calls=%async_computation.2 | async-start | bytes 1048576 | tf_op jit(solution)/shard_map/all_to_all | solution.py:21
  327.6 55.5 %reduce-scatter.6.cloned.1.call-done = bf16[64,4096]{1,0:T(8,128)(2,1)} async-done(((bf16[512,4096]{1,0:T(8,128)(2,1)}), bf16[64,4096]{1,0:T(8,128)(2,1)}) %reduce-scatter.6.cloned.1.call-update) | async-done | bytes 524304 | tf_op jit(solution)/shard_map/reduce_scatter | solution.py:19
  383.1 2.0 reshape.54
  385.1 6.5 %all-to-all-start.3 = ((bf16[16,4,4096]{2,1,0:T(4,128)(2,1)}), bf16[16,4,4096]{2,1,0:T(4,128)(2,1)}, u32[]{:S(2)}, u32[]{:S(2)}) async-start(bf16[16,4,4096]{2,1,0:T(4,128)(2,1)} %reshape.54), calls=%async_computation.5 | async-start | bytes 1048576 | tf_op jit(solution)/shard_map/all_to_all | solution.py:21
  391.6 0.3 convert_multiply_fusion
  391.9 1.3 reshape.75
  393.3 3.1 scatter_custom_fusion
  396.4 1.1 convert_element_type.41
  397.5 6.7 %all-to-all-done.3 = bf16[16,4,4096]{2,1,0:T(4,128)(2,1)} async-done(((bf16[16,4,4096]{2,1,0:T(4,128)(2,1)}), bf16[16,4,4096]{2,1,0:T(4,128)(2,1)}, u32[]{:S(2)}, u32[]{:S(2)}) %all-to-all-start.3) | async-done | bytes 524320 | tf_op jit(solution)/shard_map/all_to_all | solution.py:21
  404.1 1.1 reshape.83
  405.3 2.4 scatter_custom_fusion.1
  407.7 1.1 convert_element_type.48
  408.8 62.0 %reduce-scatter.8.cloned.1.call-done = bf16[2048,768]{0,1:T(8,128)(2,1)} async-done(((bf16[4096,768]{0,1:T(8,128)(2,1)}), bf16[2048,768]{0,1:T(8,128)(2,1)}) %reduce-scatter.8.cloned.1.call-update) | async-done | bytes 3145744 | tf_op jit(solution)/shard_map/reduce_scatter | solution.py:66
  470.8 3.2 slice_bitcast_fusion
  474.0 2.3 copy.26
  476.2 1.3 copy.25
  477.5 1.3 copy.24
  (17 shorter events, 0.1 us)
Async XLA Ops:
  7.2 1.2 copy-start
  7.2 20.4 %copy-start.7 = (f32[1,16,4]{1,2,0:T(4,128)S(1)}, f32[1,16,4]{1,2,0:T(4,128)}, u32[]{:S(2)}) copy-start(f32[1,16,4]{1,2,0:T(4,128)} %param.9) | copy-start | bytes 772
  7.2 20.5 %copy-start.2 = (bf16[128,4096]{1,0:T(8,128)(2,1)S(1)}, bf16[128,4096]{1,0:T(8,128)(2,1)}, u32[]{:S(2)}) copy-start(bf16[128,4096]{1,0:T(8,128)(2,1)} %param.13) | copy-start | bytes 3145732
  7.2 71.3 %all-gather.6.cloned.1.call-start = ((), (), s32[]{:S(2)}) async-start(), calls=%async_computation.7 | async-start | bytes 4718592 | tf_op jit(solution)/shard_map/all_gather | solution.py:13
  27.5 104.1 %all-gather.14.cloned.1.call-start = ((), (), s32[]{:S(2)}) async-start(), calls=%async_computation.12 | async-start | bytes 4718592 | tf_op jit(solution)/shard_map/all_gather | solution.py:13
  42.2 130.3 %all-gather.10.cloned.1.call-start = ((), (), s32[]{:S(2)}) async-start(), calls=%async_computation.9 | async-start | bytes 3145728 | tf_op jit(solution)/shard_map/all_gather | solution.py:34
  42.9 169.9 %all-gather.8.cloned.1.call-start = ((), (), s32[]{:S(2)}) async-start(), calls=%async_computation.8 | async-start | bytes 3145728 | tf_op jit(solution)/shard_map/all_gather | solution.py:33
  43.5 209.7 %all-gather.12.cloned.1.call-start = ((), (), s32[]{:S(2)}) async-start(), calls=%async_computation.10 | async-start | bytes 3145728 | tf_op jit(solution)/shard_map/all_gather | solution.py:35
  44.1 275.3 %reduce-scatter.4.cloned.1.call-start = ((), (), s32[]{:S(2)}) async-start(), calls=%async_computation.11 | async-start | bytes 4718592 | tf_op jit(solution)/shard_map/reduce_scatter | solution.py:19
  253.1 4.4 copy-start.6
  260.9 1.6 copy-start.5
  260.9 122.2 %reduce-scatter.6.cloned.1.call-start = ((), (), s32[]{:S(2)}) async-start(), calls=%async_computation.13 | async-start | bytes 4718592 | tf_op jit(solution)/shard_map/reduce_scatter | solution.py:19
  262.5 1.6 copy-start.4
  267.4 203.4 %reduce-scatter.8.cloned.1.call-start = ((), (), s32[]{:S(2)}) async-start(), calls=%async_computation.14 | async-start | bytes 9437184 | tf_op jit(solution)/shard_map/reduce_scatter | solution.py:66
  267.6 3.7 copy-start.3
  321.4 63.7 %all-to-all-start.1 = ((bf16[16,4,4096]{2,1,0:T(4,128)(2,1)}), bf16[16,4,4096]{2,1,0:T(4,128)(2,1)S(1)}, u32[]{:S(2)}, u32[]{:S(2)}) async-start(bf16[16,4,4096]{2,1,0:T(4,128)(2,1)} %reshape.52), calls=%async_computation.2 | async-start | bytes 1048576 | tf_op jit(solution)/shard_map/all_to_all | solution.py:21
  385.1 19.0 %all-to-all-start.3 = ((bf16[16,4,4096]{2,1,0:T(4,128)(2,1)}), bf16[16,4,4096]{2,1,0:T(4,128)(2,1)}, u32[]{:S(2)}, u32[]{:S(2)}) async-start(bf16[16,4,4096]{2,1,0:T(4,128)(2,1)} %reshape.54), calls=%async_computation.5 | async-start | bytes 1048576 | tf_op jit(solution)/shard_map/all_to_all | solution.py:21
  470.8 8.1 %copy-start.1 = (bf16[128,4096]{1,0:T(8,128)(2,1)S(1)}, bf16[128,4096]{1,0:T(8,128)(2,1)}, u32[]{:S(2)}) copy-start(bf16[128,4096]{1,0:T(8,128)(2,1)} %param.7) | copy-start | bytes 3145732
Sparse Core Ops, SparseCore 0:
  27.6 50.8 all-gather.5
  80.4 51.1 all-gather.13
  133.4 38.9 all-gather.9
  174.1 38.6 all-gather.7
  214.4 38.6 all-gather.11
  261.0 58.3 reduce-scatter.3
  321.9 61.0 reduce-scatter.5
  385.6 85.1 reduce-scatter.7
where the time goes:
time: 487 us; the launch traced here: 486 us
  waiting for transfers between devices  349 us (72%)
  local copies, waits for them, and re-layouts  32.9 us (7%)
  blocking collectives  31 us (6%)
  matrix products  26.9 us (6%)
  other arithmetic  18.5 us (4%)
  between operations  14.3 us (3%)
  starting transfers between devices  13.2 us (3%)
    reduce_scatter x2, waiting for transfers between devices, bring_back(): lax.psum_scatter(partial_value, 'col', scatter_dimension=0, tiled=True)  91.5 us
    all_gather x2, waiting for transfers between devices, send_out(): shared = lax.all_gather(arrived, 'col', axis=0, tiled=True)  80.6 us
    reduce_scatter x1, waiting for transfers between devices, shards(): lax.psum_scatter(jnp.concatenate([lax.dot_general(token_rows, gate_rows,...  62 us
    all_gather x1, waiting for transfers between devices, shards(): lax.all_gather(gate_weight, 'dp', axis=1, tiled=True)  36.2 us
    all_gather x1, waiting for transfers between devices, shards(): lax.all_gather(down_weight, 'dp', axis=1, tiled=True)  36.2 us
    all_gather x1, waiting for transfers between devices, shards(): lax.all_gather(up_weight, 'dp', axis=1, tiled=True)  33.8 us
    all_to_all x2, blocking collectives, send_out(): lax.all_to_all(payload, 'yx', split_axis=0, concat_axis=0, tiled=True)  31 us
    reshape x2, local copies, waits for them, and re-layouts, send_out(): return shared.reshape(-1, payload.shape[-1])  13.8 us
  transfers between devices with their start and end apart: 10, of which 9 were waited for; matrix products, arithmetic and copies ran while one was open for 12% of the time, Pallas kernels for 0%

commit v1 on v0

--- a/solution.py
+++ b/solution.py
@@ -29,9 +29,17 @@
     scales = gate_values[0][:, :, None]
     contract_last = (((1,), (1,)), ((), ()))
     contract_first = (((0,), (0,)), ((), ()))
+
+    def balance_slot(values):
+        mixed_arr = lax.axis_size("dp")
+        b_next = jnp.stack(mixed_arr * [values], 0)
+        opened = lax.all_to_all(b_next, "dp", 0, 0)
+        oldest = jnp.concatenate(opened, axis=1)
+        return oldest
+
     full_gate, full_up, full_down = (
         lax.all_gather(gate_weight, "dp", axis=1, tiled=True),
-        lax.all_gather(up_weight, "dp", axis=1, tiled=True),
+        balance_slot(up_weight),
         lax.all_gather(down_weight, "dp", axis=1, tiled=True),
     )
     full_gate = full_gate[0]

time: 487 us -> 460 us (0.945)
  waiting for transfers between devices: 349 us -> 317 us
    all_gather x1 -> x0, waiting for transfers between devices: 33.8 us -> none  [shards(): lax.all_gather(up_weight, 'dp', axis=1, tiled=True)]
    all_gather x2, waiting for transfers between devices: 80.6 us -> 89.3 us  [send_out(): shared = lax.all_gather(arrived, 'col', axis=0, tiled=True)]
    all_gather x1, waiting for transfers between devices: 36.2 us -> 29.6 us  [shards(): lax.all_gather(gate_weight, 'dp', axis=1, tiled=True)]
  transfers between devices with their start and end apart: 10 -> 10, of which waited for: 9 -> 8; matrix products, arithmetic and copies ran while one was open for 12% -> 14% of each run, Pallas kernels for 0% -> 0%
where the time goes in v1:
time: 460 us; the launch traced here: 459 us
  waiting for transfers between devices  317 us (69%)
  local copies, waits for them, and re-layouts  31.2 us (7%)
  blocking collectives  31 us (7%)
  matrix products  29.6 us (6%)
  other arithmetic  20 us (4%)
  starting transfers between devices  16.4 us (4%)
  between operations  14.3 us (3%)
    reduce_scatter x2, waiting for transfers between devices, bring_back(): lax.psum_scatter(partial_value, 'col', scatter_dimension=0, tiled=True)  91.9 us
    all_gather x2, waiting for transfers between devices, send_out(): shared = lax.all_gather(arrived, 'col', axis=0, tiled=True)  89.3 us
    reduce_scatter x1, waiting for transfers between devices, shards(): lax.psum_scatter(jnp.concatenate([lax.dot_general(token_rows, gate_rows,...  63.1 us
    all_gather x1, waiting for transfers between devices, shards(): lax.all_gather(down_weight, 'dp', axis=1, tiled=True)  35.4 us
    all_to_all x2, blocking collectives, send_out(): lax.all_to_all(payload, 'yx', split_axis=0, concat_axis=0, tiled=True)  31 us
    all_gather x1, waiting for transfers between devices, shards(): lax.all_gather(gate_weight, 'dp', axis=1, tiled=True)  29.6 us
    reshape x2, local copies, waits for them, and re-layouts, send_out(): return shared.reshape(-1, payload.shape[-1])  13.8 us
    all_to_all x2, starting transfers between devices, bring_back(): lax.all_to_all(summed, 'yx', split_axis=0, concat_axis=0, tiled=True)  12.1 us
  transfers between devices with their start and end apart: 10, of which 8 were waited for; matrix products, arithmetic and copies ran while one was open for 14% of the time, Pallas kernels for 0%

profile of v1, /device:TPU:1, one launch (start us, length us, event | category | flops | bytes accessed | tf_op | source)
XLA Modules:
  0.0 459.0 jit_solution(13513801458922401310)
XLA Ops:
  7.2 0.0 copy-start
  7.2 0.0 all-gather.5.cloned.1.call-start
  7.2 0.8 compare_select_fusion
  8.0 0.1 copy.22
  8.1 0.1 reshape.73
  8.2 0.2 copy-done
  8.4 0.9 gather_fusion
  9.3 0.2 reshape.56
  9.5 18.0 %all_to_all.25 = bf16[16,4,4096]{2,1,0:T(4,128)(2,1)} all-to-all(bf16[16,4,4096]{2,1,0:T(4,128)(2,1)S(1)} %reshape.56), channel_id=1, replica_groups=mesh['dp'=2,'yx'=16,'col'=8] {'yx'}, dimensions={0} | all-to-all | bytes 1048576 | tf_op jit(solution)/shard_map/all_to_all | solution.py:12
  27.5 0.0 all-gather.5.cloned.1.call-update
  27.5 0.0 all-gather.11.cloned.1.call-start
  27.6 0.1 copy.23
  27.7 0.9 gather_fusion.1
  28.5 0.3 reshape.91
  28.9 0.3 multiply_convert_fusion
  29.2 13.0 %all_to_all.26 = bf16[16,4,4096]{2,1,0:T(4,128)(2,1)} all-to-all(bf16[16,4,4096]{2,1,0:T(4,128)(2,1)S(1)} %multiply_convert_fusion), channel_id=1, replica_groups=mesh['dp'=2,'yx'=16,'col'=8] {'yx'}, dimensions={0} | all-to-all | bytes 1048576 | tf_op jit(solution)/shard_map/all_to_all | solution.py:12
  42.1 0.0 all-gather.11.cloned.1.call-update
  42.2 0.0 all-gather.7.cloned.1.call-start
  42.2 0.7 all-gather.7.cloned.1.call-update
  42.9 1.5 pad_maximum_fusion.1
  44.4 3.8 all-to-all-start.1
  48.2 0.0 all-gather.9.cloned.1.call-start
  48.2 0.5 all-gather.9.cloned.1.call-update
  48.8 0.0 reduce-scatter.4.cloned.1.call-start
  48.8 43.4 %all-gather.5.cloned.1.call-done = bf16[128,4,4096]{2,1,0:T(4,128)(2,1)} async-done(((bf16[16,4,4096]{2,1,0:T(4,128)(2,1)}), bf16[128,4,4096]{2,1,0:T(4,128)(2,1)}) %all-gather.5.cloned.1.call-update) | async-done | bytes 4194320 | tf_op jit(solution)/shard_map/all_gather | solution.py:13
  92.2 6.9 %reshape.51 = bf16[512,4096]{1,0:T(8,128)(2,1)} reshape(bf16[128,4,4096]{2,1,0:T(4,128)(2,1)} %all-gather.5.cloned.1.call-done) | data formatting | bytes 8388608 | tf_op jit(solution)/shard_map/reshape | solution.py:14
  99.1 45.9 %all-gather.11.cloned.1.call-done = bf16[128,4,4096]{2,1,0:T(4,128)(2,1)} async-done(((bf16[16,4,4096]{2,1,0:T(4,128)(2,1)}), bf16[128,4,4096]{2,1,0:T(4,128)(2,1)}) %all-gather.11.cloned.1.call-update) | async-done | bytes 4194320 | tf_op jit(solution)/shard_map/all_gather | solution.py:13
  145.0 6.9 %reshape.53 = bf16[512,4096]{1,0:T(8,128)(2,1)} reshape(bf16[128,4,4096]{2,1,0:T(4,128)(2,1)} %all-gather.11.cloned.1.call-done) | data formatting | bytes 8388608 | tf_op jit(solution)/shard_map/reshape | solution.py:14
  151.9 4.2 fusion.11
  156.2 29.6 %all-gather.7.cloned.1.call-done = bf16[1,4096,256]{2,1,0:T(8,128)(2,1)} async-done(((bf16[1,2048,256]{2,1,0:T(8,128)(2,1)}), bf16[1,4096,256]{2,1,0:T(8,128)(2,1)}) %all-gather.7.cloned.1.call-update) | async-done | bytes 2097168 | tf_op jit(solution)/shard_map/all_gather | solution.py:41
  185.8 4.9 %fusion.5 = f32[512,256]{1,0:T(8,128)} fusion(bf16[512,4096]{1,0:T(8,128)(2,1)} %reshape.51, bf16[1,4096,256]{2,1,0:T(8,128)(2,1)} %all-gather.7.cloned.1.call-done), kind=kOutput, calls=%fused_computation.16 | convolution fusion | flops 1073741824 | bytes 6815744 | tf_op jit(solution)/shard_map/dot_general | solution.py:51
  190.7 35.4 %all-gather.9.cloned.1.call-done = bf16[1,4096,256]{2,1,0:T(8,128)(2,1)} async-done(((bf16[1,2048,256]{2,1,0:T(8,128)(2,1)}), bf16[1,4096,256]{2,1,0:T(8,128)(2,1)}) %all-gather.9.cloned.1.call-update) | async-done | bytes 2097168 | tf_op jit(solution)/shard_map/all_gather | solution.py:43
  226.1 4.6 multiply_convert_fusion.1
  230.7 3.3 convolution_convert_fusion
  234.1 0.0 reduce-scatter.4.cloned.1.call-update
  234.1 0.0 reduce-scatter.6.cloned.1.call-start
  234.1 2.9 fusion.3
  237.0 3.3 add_convert_fusion
  240.3 0.0 reduce-scatter.6.cloned.1.call-update
  240.4 0.2 reduce-scatter.8.cloned.1.call-start
  240.6 3.6 convolution_convert_fusion.1
  244.3 1.4 convolution_convert_fusion.2
  245.6 1.4 convolution_convert_fusion.3
  247.0 9.4 %pad_maximum_fusion = bf16[4096,768]{0,1:T(8,128)(2,1)} fusion(bf16[4096,256]{0,1:T(8,128)(2,1)S(1)} %convolution_convert_fusion.1, bf16[4096,256]{0,1:T(8,128)(2,1)S(1)} %convolution_convert_fusion.2, bf16[4096,256]{0,1:T(8,128)(2,1)S(1)} %convolution_convert_fusion.3), kind=kLoop, calls=%fused_computation.5 | loop fusion | flops 18874368 | bytes 12582912 | tf_op jit(solution)/shard_map/concatenate | solution.py:75
  256.4 0.0 reduce-scatter.8.cloned.1.call-update
  256.4 36.2 %reduce-scatter.4.cloned.1.call-done = bf16[64,4096]{1,0:T(8,128)(2,1)} async-done(((bf16[512,4096]{1,0:T(8,128)(2,1)}), bf16[64,4096]{1,0:T(8,128)(2,1)}) %reduce-scatter.4.cloned.1.call-update) | async-done | bytes 524304 | tf_op jit(solution)/shard_map/reduce_scatter | solution.py:19
  292.6 2.0 reshape.52
  294.6 5.9 %all-to-all-start.2 = ((bf16[16,4,4096]{2,1,0:T(4,128)(2,1)}), bf16[16,4,4096]{2,1,0:T(4,128)(2,1)S(1)}, u32[]{:S(2)}, u32[]{:S(2)}) async-start(bf16[16,4,4096]{2,1,0:T(4,128)(2,1)} %reshape.52), calls=%async_computation.3 | async-start | bytes 1048576 | tf_op jit(solution)/shard_map/all_to_all | solution.py:21
  300.6 55.7 %reduce-scatter.6.cloned.1.call-done = bf16[64,4096]{1,0:T(8,128)(2,1)} async-done(((bf16[512,4096]{1,0:T(8,128)(2,1)}), bf16[64,4096]{1,0:T(8,128)(2,1)}) %reduce-scatter.6.cloned.1.call-update) | async-done | bytes 524304 | tf_op jit(solution)/shard_map/reduce_scatter | solution.py:19
  356.3 2.0 reshape.54
  358.3 6.2 %all-to-all-start.4 = ((bf16[16,4,4096]{2,1,0:T(4,128)(2,1)}), bf16[16,4,4096]{2,1,0:T(4,128)(2,1)}, u32[]{:S(2)}, u32[]{:S(2)}) async-start(bf16[16,4,4096]{2,1,0:T(4,128)(2,1)} %reshape.54), calls=%async_computation.6 | async-start | bytes 1048576 | tf_op jit(solution)/shard_map/all_to_all | solution.py:21
  364.5 0.3 convert_multiply_fusion
  364.8 1.3 reshape.75
  366.1 3.1 scatter_custom_fusion
  369.2 1.1 convert_element_type.41
  370.3 6.0 %all-to-all-done.4 = bf16[16,4,4096]{2,1,0:T(4,128)(2,1)} async-done(((bf16[16,4,4096]{2,1,0:T(4,128)(2,1)}), bf16[16,4,4096]{2,1,0:T(4,128)(2,1)}, u32[]{:S(2)}, u32[]{:S(2)}) %all-to-all-start.4) | async-done | bytes 524320 | tf_op jit(solution)/shard_map/all_to_all | solution.py:21
  376.3 1.1 reshape.83
  377.5 2.4 scatter_custom_fusion.1
  379.9 1.1 convert_element_type.48
  381.0 63.1 %reduce-scatter.8.cloned.1.call-done = bf16[2048,768]{0,1:T(8,128)(2,1)} async-done(((bf16[4096,768]{0,1:T(8,128)(2,1)}), bf16[2048,768]{0,1:T(8,128)(2,1)}) %reduce-scatter.8.cloned.1.call-update) | async-done | bytes 3145744 | tf_op jit(solution)/shard_map/reduce_scatter | solution.py:74
  444.1 3.1 slice_bitcast_fusion
  447.2 2.3 copy.26
  449.6 1.3 copy.25
  450.9 1.3 copy.24
  (15 shorter events, 0.0 us)
Async XLA Ops:
  7.2 1.2 copy-start
  7.2 85.0 %all-gather.5.cloned.1.call-start = ((), (), s32[]{:S(2)}) async-start(), calls=%async_computation.8 | async-start | bytes 4718592 | tf_op jit(solution)/shard_map/all_gather | solution.py:13
  8.4 19.2 %copy-start.6 = (f32[1,16,4]{1,2,0:T(4,128)S(1)}, f32[1,16,4]{1,2,0:T(4,128)}, u32[]{:S(2)}) copy-start(f32[1,16,4]{1,2,0:T(4,128)} %param.9) | copy-start | bytes 772
  8.4 19.2 %copy-start.2 = (bf16[128,4096]{1,0:T(8,128)(2,1)S(1)}, bf16[128,4096]{1,0:T(8,128)(2,1)}, u32[]{:S(2)}) copy-start(bf16[128,4096]{1,0:T(8,128)(2,1)} %param.13) | copy-start | bytes 3145732
  27.5 117.5 %all-gather.11.cloned.1.call-start = ((), (), s32[]{:S(2)}) async-start(), calls=%async_computation.12 | async-start | bytes 4718592 | tf_op jit(solution)/shard_map/all_gather | solution.py:13
  28.5 14.4 %copy-start.5 = (bf16[1,2048,256]{2,1,0:T(8,128)(2,1)S(1)}, bf16[1,2048,256]{2,1,0:T(8,128)(2,1)}, u32[]{:S(2)}) copy-start(bf16[1,2048,256]{2,1,0:T(8,128)(2,1)} %param.11) | copy-start | bytes 3145732
  42.2 143.6 %all-gather.7.cloned.1.call-start = ((), (), s32[]{:S(2)}) async-start(), calls=%async_computation.9 | async-start | bytes 3145728 | tf_op jit(solution)/shard_map/all_gather | solution.py:41
  44.4 107.5 %all-to-all-start.1 = ((bf16[2,1,2048,256]{3,2,1,0:T(8,128)(2,1)}), bf16[2,1,2048,256]{3,2,1,0:T(8,128)(2,1)S(1)}, u32[]{:S(2)}, u32[]{:S(2)}) async-start(bf16[2,1,2048,256]{3,2,1,0:T(8,128)(2,1)} %pad_maximum_fusion.1), calls=%async_computation.1 | async-start | bytes 4194304 | tf_op jit(solution)/shard_map/all_to_all | solution.py:36
  48.2 177.9 %all-gather.9.cloned.1.call-start = ((), (), s32[]{:S(2)}) async-start(), calls=%async_computation.10 | async-start | bytes 3145728 | tf_op jit(solution)/shard_map/all_gather | solution.py:43
  48.8 243.8 %reduce-scatter.4.cloned.1.call-start = ((), (), s32[]{:S(2)}) async-start(), calls=%async_computation.11 | async-start | bytes 4718592 | tf_op jit(solution)/shard_map/reduce_scatter | solution.py:19
  226.1 4.6 copy-start.4
  234.1 122.2 %reduce-scatter.6.cloned.1.call-start = ((), (), s32[]{:S(2)}) async-start(), calls=%async_computation.13 | async-start | bytes 4718592 | tf_op jit(solution)/shard_map/reduce_scatter | solution.py:19
  240.4 203.7 %reduce-scatter.8.cloned.1.call-start = ((), (), s32[]{:S(2)}) async-start(), calls=%async_computation.14 | async-start | bytes 9437184 | tf_op jit(solution)/shard_map/reduce_scatter | solution.py:74
  240.6 3.7 copy-start.3
  294.6 63.7 %all-to-all-start.2 = ((bf16[16,4,4096]{2,1,0:T(4,128)(2,1)}), bf16[16,4,4096]{2,1,0:T(4,128)(2,1)S(1)}, u32[]{:S(2)}, u32[]{:S(2)}) async-start(bf16[16,4,4096]{2,1,0:T(4,128)(2,1)} %reshape.52), calls=%async_computation.3 | async-start | bytes 1048576 | tf_op jit(solution)/shard_map/all_to_all | solution.py:21
  358.3 18.0 %all-to-all-start.4 = ((bf16[16,4,4096]{2,1,0:T(4,128)(2,1)}), bf16[16,4,4096]{2,1,0:T(4,128)(2,1)}, u32[]{:S(2)}, u32[]{:S(2)}) async-start(bf16[16,4,4096]{2,1,0:T(4,128)(2,1)} %reshape.54), calls=%async_computation.6 | async-start | bytes 1048576 | tf_op jit(solution)/shard_map/all_to_all | solution.py:21
  447.2 5.0 %copy-start.1 = (bf16[128,4096]{1,0:T(8,128)(2,1)S(1)}, bf16[128,4096]{1,0:T(8,128)(2,1)}, u32[]{:S(2)}) copy-start(bf16[128,4096]{1,0:T(8,128)(2,1)} %param.7) | copy-start | bytes 3145732
Sparse Core Ops, SparseCore 0:
  27.6 64.5 all-gather.4
  94.1 50.8 all-gather.10
  146.8 38.9 all-gather.6
  187.4 38.6 all-gather.8
  234.2 58.3 reduce-scatter.3
  295.0 61.2 reduce-scatter.5
  358.8 85.2 reduce-scatter.7
